TPU v7x, 32 devices: a whole 2x2x4 slice. The times are simulated.
32 devices in a mesh: subtree: 8 (over z, core), front: 4 (over y, x).
Axes of the slice: x: 2, y: 2, z: 4, core: 2. Of those that a mesh axis runs over, the one named last changes fastest.
Arguments:
- leaf_rhs: float32 [8, 2048, 256], P('subtree', 'front'), may hold values from -6 to 6
- mid_rhs: float32 [2, 4096, 256], P(None, 'front'), may hold values from -6 to 6
- root_rhs: float32 [10240, 256], P('front'), may hold values from -6 to 6
- leaf_lower: float32 [8, 2048, 2048], P('subtree', None, 'front'), may hold values from -0.125 to 0.125
- leaf_below: float32 [8, 2048, 2048], P('subtree', None, 'front'), may hold values from -0.125 to 0.125
- leaf_right: float32 [8, 2048, 2048], P('subtree', None, 'front'), may hold values from -0.125 to 0.125
- leaf_upper: float32 [8, 2048, 2048], P('subtree', None, 'front'), may hold values from -0.125 to 0.125
- mid_lower: float32 [2, 4096, 4096], P(None, 'subtree', 'front'), may hold values from -0.09375 to 0.09375
- mid_below: float32 [2, 4096, 4096], P(None, 'front', 'subtree'), may hold values from -0.09375 to 0.09375
- mid_right: float32 [2, 4096, 4096], P(None, 'subtree', 'front'), may hold values from -0.09375 to 0.09375
- mid_upper: float32 [2, 4096, 4096], P(None, 'front', 'subtree'), may hold values from -0.09375 to 0.09375
- root_lower: float32 [10240, 10240], P('subtree', 'front'), may hold values from -0.0625 to 0.0625
- root_upper: float32 [10240, 10240], P('front', 'subtree'), may hold values from -0.0625 to 0.0625
- leaf_parent: int32 [8], replicated, may hold values from 0 to 1, as said below
- leaf_sizes: int32 [8], replicated, may hold values from 1024 to 2048, as said below
- leaf_map: int32 [8, 16], replicated, may hold values from 0 to 63, as said below
- mid_map: int32 [2, 32], replicated, may hold values from 0 to 79, as said below
Outputs:
- leaf_sol: float32 [8, 2048, 256], P('subtree', 'front')
- mid_sol: float32 [2, 4096, 256], P(None, 'front')
- root_sol: float32 [10240, 256], P('front')
Inputs may be any that keep to these rules, and one draw needn't show every extreme that they name: `leaf_parent`: every level-1 front is the parent of at least one lowest-level front. `leaf_sizes`: a multiple of 128; some front has all 2048 rows live. `leaf_map`: a front's blocks go to distinct parent blocks; update block b of a lowest-level front, with c = b // 4, goes to c * 8 + i or to that plus 4096 / 128, for some i with 0 <= i < 8. `mid_map`: a front's blocks go to distinct root blocks; update block b of a level-1 front, with c = b // 8, goes to c * 20 + i for some i with 0 <= i < 20.
All inputs are finite; a program needn't handle non-finite values.
Results may differ from a plain program's by a relative error of at most 0.00013.
Values sent between devices are 32-bit elements; how exact they have to be, the bound alone decides.
No kernel may reach another device: no remote copies, remote signals or barrier semaphores. Data moves between devices by JAX's collectives and lax.ppermute only.
A program may use at most 128 MiB of HBM per device.

v0:
```python
import jax
import jax.numpy as jnp
from jax import lax
from jax.sharding import PartitionSpec as P

MID_PIV = 4096
BLOCK = 128


def leaf_product(matrix, vector):
    return lax.psum_scatter(
        jnp.dot(
            matrix, vector, preferred_element_type=jnp.float32, precision=lax.Precision.HIGHEST
        ),
        "front",
        scatter_dimension=0,
        tiled=True,
    )


def across_front(partial_value):
    return lax.psum(partial_value, "front")


def across_subtree(partial_value):
    return lax.psum(partial_value, "subtree")


def batched(matrix, vector):
    return jnp.einsum(
        "fab,fbr->far",
        matrix,
        vector,
        preferred_element_type=jnp.float32,
        precision=lax.Precision.HIGHEST,
    )


def leaf_select(parents, blocks, fronts, column, width):
    front_ids = jnp.arange(fronts, dtype=jnp.int32)[:, None, None, None, None]
    halves = jnp.arange(2, dtype=jnp.int32)[None, :, None, None, None]
    slots = jnp.arange(width, dtype=jnp.int32)[None, None, :, None, None]
    target = halves * (MID_PIV // BLOCK) + column * width + slots
    match_parent = parents[None, None, None, :, None] == front_ids
    match_block = blocks[None, None, None, :, :] == target
    return (match_parent & match_block).astype(jnp.float32)


def on_device(
    leaf_rhs,
    mid_rhs,
    root_rhs,
    leaf_lower,
    leaf_below,
    leaf_right,
    leaf_upper,
    mid_lower,
    mid_below,
    mid_right,
    mid_upper,
    root_lower,
    root_upper,
    leaf_parent,
    leaf_sizes,
    leaf_map,
    mid_map,
):
    group = lax.axis_index("subtree")
    column = lax.axis_index("front")
    local_rows = leaf_rhs.shape[1]
    scenarios = leaf_rhs.shape[2]
    leaf_width = local_rows // BLOCK
    fronts = mid_rhs.shape[0]
    mid_width = mid_rhs.shape[1] // BLOCK
    root_width = root_rhs.shape[0] // BLOCK
    own_size = lax.dynamic_slice_in_dim(leaf_sizes, group, 1)
    positions = column * local_rows + jnp.arange(local_rows, dtype=jnp.int32)
    live = (positions < own_size[0]).astype(jnp.float32)[:, None]
    leaf_fwd = live * leaf_product(leaf_lower[0], live * leaf_rhs[0])
    leaf_contrib = -leaf_product(leaf_below[0], leaf_fwd)
    own_parent = lax.dynamic_slice_in_dim(leaf_parent, group, 1)
    own_blocks = lax.dynamic_slice(leaf_map, (group, column * leaf_width), (1, leaf_width))
    own_select = leaf_select(own_parent, own_blocks, fronts, column, mid_width)
    column_blocks = lax.dynamic_slice_in_dim(leaf_map, column * leaf_width, leaf_width, 1)
    selection = leaf_select(leaf_parent, column_blocks, fronts, column, mid_width)
    piece = lax.all_gather(leaf_contrib[None], "subtree", axis=0, tiled=True)
    shaped = piece.reshape(piece.shape[0], leaf_width, BLOCK, scenarios)
    assembled = jnp.einsum(
        "phqgk,gkbr->phqbr",
        selection,
        shaped,
        preferred_element_type=jnp.float32,
        precision=lax.Precision.HIGHEST,
    )
    mid_pivot = mid_rhs + assembled[:, 0].reshape(fronts, mid_width * BLOCK, scenarios)
    mid_update = assembled[:, 1].reshape(fronts, mid_width * BLOCK, scenarios)
    mid_fwd = across_front(batched(mid_lower, mid_pivot))
    mid_contrib = mid_update - across_subtree(batched(mid_below, mid_fwd))
    column_map = lax.dynamic_slice_in_dim(mid_map, column * mid_width, mid_width, 1)
    slots = jnp.arange(root_width, dtype=jnp.int32)[:, None, None]
    root_select = (column_map[None, :, :] == column * root_width + slots).astype(jnp.float32)
    root_added = jnp.einsum(
        "qpk,pkbr->qbr",
        root_select,
        mid_contrib.reshape(fronts, mid_width, BLOCK, scenarios),
        preferred_element_type=jnp.float32,
        precision=lax.Precision.HIGHEST,
    )
    root_start = root_rhs + root_added.reshape(root_width * BLOCK, scenarios)
    root_fwd = across_front(
        jnp.dot(
            root_lower,
            root_start,
            preferred_element_type=jnp.float32,
            precision=lax.Precision.HIGHEST,
        )
    )
    root_sol = across_subtree(
        jnp.dot(
            root_upper,
            root_fwd,
            preferred_element_type=jnp.float32,
            precision=lax.Precision.HIGHEST,
        )
    )
    mid_ext = jnp.einsum(
        "qpk,qbr->pkbr",
        root_select,
        root_sol.reshape(root_width, BLOCK, scenarios),
        preferred_element_type=jnp.float32,
        precision=lax.Precision.HIGHEST,
    )
    mid_ext = mid_ext.reshape(fronts, mid_width * BLOCK, scenarios)
    mid_back = mid_fwd - across_front(batched(mid_right, mid_ext))
    mid_sol = across_subtree(batched(mid_upper, mid_back))
    whole_column = jnp.stack(
        [
            mid_sol.reshape(fronts, mid_width, BLOCK, scenarios),
            mid_ext.reshape(fronts, mid_width, BLOCK, scenarios),
        ],
        axis=1,
    )
    leaf_ext = jnp.einsum(
        "phqgk,phqbr->gkbr",
        own_select,
        whole_column,
        preferred_element_type=jnp.float32,
        precision=lax.Precision.HIGHEST,
    )
    leaf_ext = leaf_ext.reshape(local_rows, scenarios)
    leaf_back = live * (leaf_fwd - leaf_product(leaf_right[0], leaf_ext))
    leaf_sol = live * leaf_product(leaf_upper[0], leaf_back)
    return (leaf_sol[None], mid_sol, root_sol)


def solution(mesh):
    return jax.shard_map(
        on_device,
        mesh=mesh,
        in_specs=(
            P("subtree", "front", None),
            P(None, "front", None),
            P("front", None),
            P("subtree", None, "front"),
            P("subtree", None, "front"),
            P("subtree", None, "front"),
            P("subtree", None, "front"),
            P(None, "subtree", "front"),
            P(None, "front", "subtree"),
            P(None, "subtree", "front"),
            P(None, "front", "subtree"),
            P("subtree", "front"),
            P("front", "subtree"),
            P(),
            P(),
            P(),
            P(),
        ),
        out_specs=(P("subtree", "front", None), P(None, "front", None), P("front", None)),
        check_vma=False,
    )
```

profile of v0, /device:TPU:0, one launch (start us, length us, event | category | flops | bytes accessed | tf_op | source)
XLA Modules:
  0.0 725.7 jit_solution(1965828273986753131)
XLA Ops:
  7.2 1.2 dynamic_slice.15
  8.5 0.6 fusion.57
  9.1 10.6 %fusion.15 = f32[2048,256]{0,1:T(8,128)} fusion(f32[1,2048,512]{2,1,0:T(8,128)} %param.20, f32[1,512,256]{2,1,0:T(8,128)} %param.17, f32[512]{0:T(512)S(1)} %fusion.57), kind=kOutput, calls=%fused_computation.16 | convolution fusion | flops 3221356544 | bytes 6817792 | tf_op jit(solution)/shard_map/dot_general | solution.py:12
  19.8 38.0 %reduce-scatter.5.cloned.1.call-done = f32[512,256]{0,1:T(8,128)} async-done(((f32[2048,256]{0,1:T(8,128)}), f32[512,256]{0,1:T(8,128)}) %reduce-scatter.5.cloned.1.call-update) | async-done | bytes 524304 | tf_op jit(solution)/shard_map/reduce_scatter | solution.py:11
  57.8 7.3 %fusion.18 = f32[2048,256]{0,1:T(8,128)} fusion(f32[1,2048,512]{2,1,0:T(8,128)} %param.21, f32[512,256]{0,1:T(8,128)} %reduce-scatter.5.cloned.1.call-done, f32[512]{0:T(512)S(1)} %fusion.57), kind=kOutput, calls=%fused_computation.17 | convolution fusion | flops 3221356544 | bytes 6817792 | tf_op jit(solution)/shard_map/dot_general | solution.py:12
  65.2 35.3 %reduce-scatter.7.cloned.1.call-done = f32[512,256]{0,1:T(8,128)} async-done(((f32[2048,256]{0,1:T(8,128)}), f32[512,256]{0,1:T(8,128)}) %reduce-scatter.7.cloned.1.call-update) | async-done | bytes 524304 | tf_op jit(solution)/shard_map/reduce_scatter | solution.py:11
  100.5 1.9 neg.3
  102.4 0.2 all-reduce.7.cloned.1.call-start
  102.6 0.1 constant_dynamic-slice_fusion.1
  102.7 0.1 copy.29
  102.8 0.1 iota_add_fusion
  102.8 0.1 broadcast_compare_fusion
  102.9 46.6 %all-gather.3.cloned.1.call-done = f32[4096,256]{0,1:T(8,128)} async-done(((f32[512,256]{0,1:T(8,128)}), f32[4096,256]{0,1:T(8,128)}) %all-gather.3.cloned.1.call-update) | async-done | bytes 4194320 | tf_op jit(solution)/shard_map/all_gather | solution.py:86
  149.5 6.0 reshape.127
  155.6 6.6 copy.48
  162.2 6.1 convolution_bitcast_fusion.2
  168.3 0.4 fusion.59
  168.6 0.6 copy.31
  169.3 0.6 copy-done.6
  169.8 1.3 copy-done.2
  171.2 8.0 %fusion.29 = f32[2,512,256]{1,2,0:T(8,128)} fusion(f32[2,512,1024]{2,1,0:T(8,128)S(1)} %copy-done.2, f32[2,1024,256]{2,1,0:T(8,128)S(1)} %copy-done.6, f32[2,1024,256]{2,1,0:T(8,128)S(1)} %bitcast.122), kind=kOutput, calls=%fused_computation.28 | convolution fusion | flops 3221749760 | bytes 9437184 | tf_op jit(solution)/shard_map/fab,fbr->far/dot_general | solution.py:30
  179.2 0.3 all-reduce.9.cloned.1.call-start
  179.4 51.2 %all-reduce.7.cloned.1.call-done = f32[2,512,256]{1,2,0:T(8,128)} async-done(((f32[2,512,256]{1,2,0:T(8,128)}), f32[2,512,256]{1,2,0:T(8,128)}) %all-reduce.7.cloned.1.call-update) | async-done | bytes 1048592 | tf_op jit(solution)/shard_map/psum | solution.py:22
  230.6 7.5 %convolution_bitcast_fusion.5 = f32[2,1024,256]{1,2,0:T(8,128)} fusion(f32[2,512,256]{1,2,0:T(8,128)} %all-reduce.7.cloned.1.call-done, f32[2,1024,512]{2,1,0:T(8,128)} %param.25), kind=kOutput, calls=%fused_computation.27 | convolution fusion | flops 3221225472 | bytes 7340032 | tf_op jit(solution)/shard_map/fab,fbr->far/dot_general | solution.py:30
  238.2 0.1 constant_dynamic-slice_fusion
  238.3 1.9 copy.33
  240.2 1.9 copy.34
  242.1 61.3 %all-reduce.9.cloned.1.call-done = f32[2,1024,256]{1,2,0:T(8,128)} async-done(((f32[2,1024,256]{1,2,0:T(8,128)}), f32[2,1024,256]{1,2,0:T(8,128)}) %all-reduce.9.cloned.1.call-update) | async-done | bytes 2097168 | tf_op jit(solution)/shard_map/psum | solution.py:26
  303.4 2.1 sub.9
  305.5 0.5 copy.59
  305.9 2.0 copy.35
  308.0 3.2 convolution_bitcast_fusion.3
  311.2 0.8 copy.36
  312.0 0.9 copy-done.5
  312.9 0.3 bitcast_add_fusion
  313.2 26.2 %convolution_bitcast_fusion.1 = f32[1280,256]{0,1:T(8,128)} fusion(f32[2560,256]{1,0:T(8,128)S(1)} %bitcast_add_fusion, f32[1280,2560]{1,0:T(8,128)} %param.28), kind=kOutput, calls=%fused_computation.20 | convolution fusion | flops 10066329600 | bytes 17039360 | tf_op jit(solution)/shard_map/dot_general | solution.py:111
  339.5 56.1 %all-reduce.11.cloned.1.call-done = f32[1280,256]{0,1:T(8,128)} async-done(((f32[1280,256]{0,1:T(8,128)}), f32[1280,256]{0,1:T(8,128)}) %all-reduce.11.cloned.1.call-update) | async-done | bytes 1310736 | tf_op jit(solution)/shard_map/psum | solution.py:22
  395.6 15.6 %convolution_bitcast_fusion = f32[2560,256]{0,1:T(8,128)} fusion(f32[1280,256]{0,1:T(8,128)} %all-reduce.11.cloned.1.call-done, f32[2560,1280]{1,0:T(8,128)} %param.29), kind=kOutput, calls=%fused_computation.12 | convolution fusion | flops 10066329600 | bytes 17039360 | tf_op jit(solution)/shard_map/dot_general | solution.py:119
  411.3 69.2 %all-reduce.13.cloned.1.call-done = f32[2560,256]{0,1:T(8,128)} async-done(((f32[2560,256]{0,1:T(8,128)}), f32[2560,256]{0,1:T(8,128)}) %all-reduce.13.cloned.1.call-update) | async-done | bytes 2621456 | tf_op jit(solution)/shard_map/psum | solution.py:26
  480.5 3.2 copy.37
  483.7 4.4 fusion.12
  488.1 0.6 copy.39
  488.7 1.5 copy-done.1
  490.3 8.0 %convolution_bitcast_fusion.6 = f32[2,512,256]{1,2,0:T(8,128)} fusion(f32[2,1024,256]{2,1,0:T(8,128)S(1)} %bitcast.118, f32[2,512,1024]{2,1,0:T(8,128)S(1)} %copy-done.1), kind=kOutput, calls=%fused_computation.29 | convolution fusion | flops 3221225472 | bytes 7340032 | tf_op jit(solution)/shard_map/fab,fbr->far/dot_general | solution.py:30
  498.3 0.3 all-reduce.17.cloned.1.call-start
  498.6 51.4 %all-reduce.15.cloned.1.call-done = f32[2,512,256]{1,2,0:T(8,128)} async-done(((f32[2,512,256]{1,2,0:T(8,128)}), f32[2,512,256]{1,2,0:T(8,128)}) %all-reduce.15.cloned.1.call-update) | async-done | bytes 1048592 | tf_op jit(solution)/shard_map/psum | solution.py:22
  550.0 7.5 %convolution_bitcast_fusion.4 = f32[2,1024,256]{1,2,0:T(8,128)} fusion(f32[2,1024,512]{2,1,0:T(8,128)} %param.27, f32[2,512,256]{1,2,0:T(8,128)S(1)} %copy-done.4, f32[2,512,256]{1,2,0:T(8,128)} %all-reduce.15.cloned.1.call-done), kind=kOutput, calls=%fused_computation.26 | convolution fusion | flops 3221487616 | bytes 8388608 | tf_op jit(solution)/shard_map/fab,fbr->far/dot_general | solution.py:30
  557.6 0.6 dynamic_slice.16
  558.2 0.1 dynamic-slice_bitcast_fusion
  558.2 0.6 iota_compare_fusion.1
  558.9 0.1 broadcast_compare_fusion.1
  559.0 63.8 %all-reduce.17.cloned.1.call-done = f32[2,1024,256]{1,2,0:T(8,128)} async-done(((f32[2,1024,256]{1,2,0:T(8,128)}), f32[2,1024,256]{1,2,0:T(8,128)}) %all-reduce.17.cloned.1.call-update) | async-done | bytes 2097168 | tf_op jit(solution)/shard_map/psum | solution.py:26
  622.8 2.9 copy.40
  625.6 2.8 copy.41
  628.5 1.9 fusion.32
  630.4 0.1 copy.43
  630.5 0.1 copy-done.3
  630.6 8.4 %fusion.21 = f32[2048,256]{0,1:T(8,128)} fusion(f32[512,256]{1,0:T(8,128)S(1)} %bitcast.123, f32[1,2048,512]{2,1,0:T(8,128)S(1)} %copy-done.3), kind=kOutput, calls=%fused_computation.18 | convolution fusion | flops 3221225472 | bytes 6815744 | tf_op jit(solution)/shard_map/dot_general | solution.py:12
  639.0 0.3 reduce-scatter.11.cloned.1.call-start
  639.3 34.6 %reduce-scatter.9.cloned.1.call-done = f32[512,256]{0,1:T(8,128)} async-done(((f32[2048,256]{0,1:T(8,128)}), f32[512,256]{0,1:T(8,128)}) %reduce-scatter.9.cloned.1.call-update) | async-done | bytes 524304 | tf_op jit(solution)/shard_map/reduce_scatter | solution.py:11
  674.0 7.4 %fusion.24 = f32[2048,256]{0,1:T(8,128)} fusion(f32[1,2048,512]{2,1,0:T(8,128)} %param.23, f32[512,256]{0,1:T(8,128)} %reduce-scatter.9.cloned.1.call-done, f32[512,256]{0,1:T(8,128)S(1)} %copy-done.7, f32[512]{0:T(512)S(1)} %fusion.57), kind=kOutput, calls=%fused_computation.19 | convolution fusion | flops 3221618688 | bytes 7342080 | tf_op jit(solution)/shard_map/dot_general | solution.py:12
  681.3 35.3 %reduce-scatter.11.cloned.1.call-done = f32[512,256]{0,1:T(8,128)} async-done(((f32[2048,256]{0,1:T(8,128)}), f32[512,256]{0,1:T(8,128)}) %reduce-scatter.11.cloned.1.call-update) | async-done | bytes 524304 | tf_op jit(solution)/shard_map/reduce_scatter | solution.py:11
  716.7 1.1 multiply_bitcast_fusion
  717.8 1.0 copy.44
  (36 shorter events, 0.5 us)
Async XLA Ops:
  7.2 95.4 %copy-start = (s32[8,16]{1,0:T(8,128)S(1)}, s32[8,16]{1,0:T(8,128)}, u32[]{:S(2)}) copy-start(s32[8,16]{1,0:T(8,128)} %param.32) | copy-start | bytes 1540
  7.2 50.6 %reduce-scatter.5.cloned.1.call-start = ((), (), s32[]{:S(2)}) async-start(), calls=%async_computation.4 | async-start | bytes 2621440 | tf_op jit(solution)/shard_map/reduce_scatter | solution.py:11
  19.7 80.7 %reduce-scatter.7.cloned.1.call-start = ((), (), s32[]{:S(2)}) async-start(), calls=%async_computation.5 | async-start | bytes 2621440 | tf_op jit(solution)/shard_map/reduce_scatter | solution.py:11
  65.1 37.7 %copy-start.9 = (s32[8]{0:T(128)S(1)}, s32[8]{0:T(128)}, u32[]{:S(2)}) copy-start(s32[8]{0:T(128)} %param.30) | copy-start | bytes 100
  65.1 84.4 %all-gather.3.cloned.1.call-start = ((), (), s32[]{:S(2)}) async-start(), calls=%async_computation.14 | async-start | bytes 4718592 | tf_op jit(solution)/shard_map/all_gather | solution.py:86
  102.4 128.2 %all-reduce.7.cloned.1.call-start = ((), (), s32[]{:S(2)}) async-start(), calls=%async_computation.6 | async-start | bytes 2097152 | tf_op jit(solution)/shard_map/psum | solution.py:22
  168.3 1.6 copy-start.6
  168.6 2.5 copy-start.2
  179.2 59.0 %copy-start.8 = (s32[2,32]{1,0:T(2,128)S(1)}, s32[2,32]{1,0:T(2,128)}, u32[]{:S(2)}) copy-start(s32[2,32]{1,0:T(2,128)} %param.33) | copy-start | bytes 772
  179.2 124.2 %all-reduce.9.cloned.1.call-start = ((), (), s32[]{:S(2)}) async-start(), calls=%async_computation.7 | async-start | bytes 4194304 | tf_op jit(solution)/shard_map/psum | solution.py:26
  238.1 157.4 %all-reduce.11.cloned.1.call-start = ((), (), s32[]{:S(2)}) async-start(), calls=%async_computation.8 | async-start | bytes 2621440 | tf_op jit(solution)/shard_map/psum | solution.py:22
  311.2 1.7 copy-start.5
  339.4 141.1 %all-reduce.13.cloned.1.call-start = ((), (), s32[]{:S(2)}) async-start(), calls=%async_computation.9 | async-start | bytes 5242880 | tf_op jit(solution)/shard_map/psum | solution.py:26
  411.2 138.8 %all-reduce.15.cloned.1.call-start = ((), (), s32[]{:S(2)}) async-start(), calls=%async_computation.10 | async-start | bytes 2097152 | tf_op jit(solution)/shard_map/psum | solution.py:22
  488.1 2.2 copy-start.1
  490.3 59.8 %copy-start.4 = (f32[2,512,256]{1,2,0:T(8,128)S(1)}, f32[2,512,256]{1,2,0:T(8,128)}, u32[]{:S(2)}) copy-start(f32[2,512,256]{1,2,0:T(8,128)} %all-reduce.7.cloned.1.call-done) | copy-start | bytes 3145732
  498.3 124.4 %all-reduce.17.cloned.1.call-start = ((), (), s32[]{:S(2)}) async-start(), calls=%async_computation.11 | async-start | bytes 4194304 | tf_op jit(solution)/shard_map/psum | solution.py:26
  557.5 116.4 %reduce-scatter.9.cloned.1.call-start = ((), (), s32[]{:S(2)}) async-start(), calls=%async_computation.12 | async-start | bytes 2621440 | tf_op jit(solution)/shard_map/reduce_scatter | solution.py:11
  628.5 2.2 copy-start.3
  630.6 43.3 %copy-start.7 = (f32[512,256]{0,1:T(8,128)S(1)}, f32[512,256]{0,1:T(8,128)}, u32[]{:S(2)}) copy-start(f32[512,256]{0,1:T(8,128)} %reduce-scatter.5.cloned.1.call-done) | copy-start | bytes 1572868
  639.0 77.7 %reduce-scatter.11.cloned.1.call-start = ((), (), s32[]{:S(2)}) async-start(), calls=%async_computation.13 | async-start | bytes 2621440 | tf_op jit(solution)/shard_map/reduce_scatter | solution.py:11
Sparse Core Ops, SparseCore 0:
  19.8 37.9 reduce-scatter.4
  65.2 35.1 reduce-scatter.6
  102.6 46.8 all-gather.2
  179.3 51.2 all-reduce.6
  238.2 65.1 all-reduce.8
  339.6 55.9 all-reduce.10
  411.3 69.0 all-reduce.12
  498.4 51.5 all-reduce.14
  557.6 65.0 all-reduce.16
  639.1 34.7 reduce-scatter.8
  681.5 35.1 reduce-scatter.10
where the time goes:
time: 734 us; the launch traced here: 726 us
  waiting for transfers between devices  543 us (74%)
  matrix products  122 us (17%)
  local copies, waits for them, and re-layouts  38.1 us (5%)
  between operations  14.5 us (2%)
    psum x3, waiting for transfers between devices, across_subtree(): return lax.psum(partial_value, 'subtree')  194 us
    psum x3, waiting for transfers between devices, across_front(): return lax.psum(partial_value, 'front')  159 us
    reduce_scatter x4, waiting for transfers between devices, leaf_product(): lax.psum_scatter(jnp.dot(matrix, vector, preferred_element_type=jnp.float...  143 us
    all_gather x1, waiting for transfers between devices, on_device(): piece = lax.all_gather(leaf_contrib[None], 'subtree', axis=0, tiled=True)  46.6 us
    dot_general x4, matrix products, leaf_product(): jnp.dot(matrix, vector, preferred_element_type=jnp.float32, precision=lax...  33.6 us
    dot_general x4, matrix products, batched(): jnp.einsum('fab,fbr->far', matrix, vector, preferred_element_type=jnp.flo...  31 us
    dot_general x1, matrix products, on_device(): jnp.dot(root_lower, root_start, preferred_element_type=jnp.float32, preci...  26.2 us
    dot_general x1, matrix products, on_device(): jnp.dot(root_upper, root_fwd, preferred_element_type=jnp.float32, precisi...  15.6 us
  transfers between devices with their start and end apart: 11, of which 11 were waited for; matrix products, arithmetic and copies ran while one was open for 1% of the time, Pallas kernels for 0%

commit v1 on v0

--- a/solution.py
+++ b/solution.py
@@ -83,7 +83,14 @@
     own_select = leaf_select(own_parent, own_blocks, fronts, column, mid_width)
     column_blocks = lax.dynamic_slice_in_dim(leaf_map, column * leaf_width, leaf_width, 1)
     selection = leaf_select(leaf_parent, column_blocks, fronts, column, mid_width)
-    piece = lax.all_gather(leaf_contrib[None], "subtree", axis=0, tiled=True)
+    ring = [leaf_contrib[None]]
+    for hop in range(7):
+        ring.append(lax.ppermute(ring[-1], "subtree", [(dev, (dev + 1) % 8) for dev in range(8)]))
+    piece = jnp.roll(
+        jnp.concatenate(ring[::-1], axis=0),
+        (lax.axis_index("subtree") + 1) * ring[0].shape[0],
+        axis=0,
+    )
     shaped = piece.reshape(piece.shape[0], leaf_width, BLOCK, scenarios)
     assembled = jnp.einsum(
         "phqgk,gkbr->phqbr",

time: 734 us -> 759 us (1.034)
  waiting for transfers between devices: 543 us -> 568 us
    ppermute x0 -> x7, waiting for transfers between devices: none -> 72.8 us  [on_device(): lax.ppermute(ring[-1], 'subtree', [(dev, (dev + 1) % 8) for dev in range(...]
    all_gather x1 -> x0, waiting for transfers between devices: 46.6 us -> none  [on_device(): piece = lax.all_gather(leaf_contrib[None], 'subtree', axis=0, tiled=True)]
    reshape x2 -> x0, local copies, waits for them, and re-layouts: 12.6 us -> none  [on_device(): shaped = piece.reshape(piece.shape[0], leaf_width, BLOCK, scenarios)]
    dynamic_slice x0 -> x2, local copies, waits for them, and re-layouts: none -> 8.28 us  [on_device(): jnp.roll(jnp.concatenate(ring[::-1], axis=0), (lax.axis_index('subtree')...]
  transfers between devices with their start and end apart: 11 -> 17, of which waited for: 11 -> 17; matrix products, arithmetic and copies ran while one was open for 1% -> 1% of each run, Pallas kernels for 0% -> 0%
where the time goes in v1:
time: 759 us; the launch traced here: 749 us
  waiting for transfers between devices  568 us (75%)
  matrix products  125 us (16%)
  local copies, waits for them, and re-layouts  34.8 us (5%)
  between operations  15 us (2%)
    psum x3, waiting for transfers between devices, across_subtree(): return lax.psum(partial_value, 'subtree')  194 us
    psum x3, waiting for transfers between devices, across_front(): return lax.psum(partial_value, 'front')  157 us
    reduce_scatter x4, waiting for transfers between devices, leaf_product(): lax.psum_scatter(jnp.dot(matrix, vector, preferred_element_type=jnp.float...  143 us
    ppermute x7, waiting for transfers between devices, on_device(): lax.ppermute(ring[-1], 'subtree', [(dev, (dev + 1) % 8) for dev in range(...  72.8 us
    dot_general x4, matrix products, leaf_product(): jnp.dot(matrix, vector, preferred_element_type=jnp.float32, precision=lax...  33.6 us
    dot_general x4, matrix products, batched(): jnp.einsum('fab,fbr->far', matrix, vector, preferred_element_type=jnp.flo...  31.2 us
    dot_general x1, matrix products, on_device(): jnp.dot(root_lower, root_start, preferred_element_type=jnp.float32, preci...  26.2 us
    dot_general x1, matrix products, on_device(): jnp.dot(root_upper, root_fwd, preferred_element_type=jnp.float32, precisi...  15.6 us
  transfers between devices with their start and end apart: 17, of which 17 were waited for; matrix products, arithmetic and copies ran while one was open for 1% of the time, Pallas kernels for 0%

profile of v1, /device:TPU:0, one launch (start us, length us, event | category | flops | bytes accessed | tf_op | source)
XLA Modules:
  0.0 749.2 jit_solution(12197424802115103946)
XLA Ops:
  7.2 1.2 dynamic_slice.19
  8.5 0.6 fusion.62
  9.1 10.6 %fusion.17 = f32[2048,256]{0,1:T(8,128)} fusion(f32[1,2048,512]{2,1,0:T(8,128)} %param.20, f32[1,512,256]{2,1,0:T(8,128)} %param.17, f32[512]{0:T(512)S(1)} %fusion.62), kind=kOutput, calls=%fused_computation.18 | convolution fusion | flops 3221356544 | bytes 6817792 | tf_op jit(solution)/shard_map/dot_general | solution.py:12
  19.8 38.0 %reduce-scatter.5.cloned.1.call-done = f32[512,256]{0,1:T(8,128)} async-done(((f32[2048,256]{0,1:T(8,128)}), f32[512,256]{0,1:T(8,128)}) %reduce-scatter.5.cloned.1.call-update) | async-done | bytes 524304 | tf_op jit(solution)/shard_map/reduce_scatter | solution.py:11
  57.8 7.3 fusion.20
  65.2 35.3 %reduce-scatter.7.cloned.1.call-done = f32[512,256]{0,1:T(8,128)} async-done(((f32[2048,256]{0,1:T(8,128)}), f32[512,256]{0,1:T(8,128)}) %reduce-scatter.7.cloned.1.call-update) | async-done | bytes 524304 | tf_op jit(solution)/shard_map/reduce_scatter | solution.py:11
  100.5 1.2 negate_bitcast_fusion
  101.7 10.4 %collective-permute-done = f32[1,512,256]{1,2,0:T(8,128)S(1)} collective-permute-done((f32[1,512,256]{1,2,0:T(8,128)S(1)}, f32[1,512,256]{1,2,0:T(8,128)S(1)}, u32[]{:S(2)}, u32[]{:S(2)}) %collective-permute-start) | collective-permute-done | bytes 524320 | tf_op jit(solution)/shard_map/ppermute | solution.py:88
  112.1 10.4 %collective-permute-done.1 = f32[1,512,256]{1,2,0:T(8,128)S(1)} collective-permute-done((f32[1,512,256]{1,2,0:T(8,128)S(1)}, f32[1,512,256]{1,2,0:T(8,128)S(1)}, u32[]{:S(2)}, u32[]{:S(2)}) %collective-permute-start.1) | collective-permute-done | bytes 524320 | tf_op jit(solution)/shard_map/ppermute | solution.py:88
  122.5 10.4 %collective-permute-done.2 = f32[1,512,256]{1,2,0:T(8,128)S(1)} collective-permute-done((f32[1,512,256]{1,2,0:T(8,128)S(1)}, f32[1,512,256]{1,2,0:T(8,128)S(1)}, u32[]{:S(2)}, u32[]{:S(2)}) %collective-permute-start.2) | collective-permute-done | bytes 524320 | tf_op jit(solution)/shard_map/ppermute | solution.py:88
  132.9 10.4 %collective-permute-done.3 = f32[1,512,256]{1,2,0:T(8,128)S(1)} collective-permute-done((f32[1,512,256]{1,2,0:T(8,128)S(1)}, f32[1,512,256]{1,2,0:T(8,128)S(1)}, u32[]{:S(2)}, u32[]{:S(2)}) %collective-permute-start.3) | collective-permute-done | bytes 524320 | tf_op jit(solution)/shard_map/ppermute | solution.py:88
  143.3 10.4 %collective-permute-done.4 = f32[1,512,256]{1,2,0:T(8,128)S(1)} collective-permute-done((f32[1,512,256]{1,2,0:T(8,128)S(1)}, f32[1,512,256]{1,2,0:T(8,128)S(1)}, u32[]{:S(2)}, u32[]{:S(2)}) %collective-permute-start.4) | collective-permute-done | bytes 524320 | tf_op jit(solution)/shard_map/ppermute | solution.py:88
  153.8 0.1 copy.28
  153.9 10.3 %collective-permute-done.5 = f32[1,512,256]{1,2,0:T(8,128)} collective-permute-done((f32[1,512,256]{1,2,0:T(8,128)S(1)}, f32[1,512,256]{1,2,0:T(8,128)}, u32[]{:S(2)}, u32[]{:S(2)}) %collective-permute-start.5) | collective-permute-done | bytes 524320 | tf_op jit(solution)/shard_map/ppermute | solution.py:88
  164.3 0.1 broadcast_compare_fusion
  164.4 10.5 %collective-permute-done.6 = f32[1,512,256]{1,2,0:T(8,128)S(1)} collective-permute-done((f32[1,512,256]{1,2,0:T(8,128)}, f32[1,512,256]{1,2,0:T(8,128)S(1)}, u32[]{:S(2)}, u32[]{:S(2)}) %collective-permute-start.6) | collective-permute-done | bytes 524320 | tf_op jit(solution)/shard_map/ppermute | solution.py:88
  174.9 1.1 constant_dynamic-update-slice_fusion.14
  176.3 1.1 constant_dynamic-update-slice_fusion.6
  177.6 2.7 constant_dynamic-slice_fusion.1
  180.3 5.6 copy.29
  185.9 8.3 %fusion.29 = f32[2,2,8,128,256]{4,2,3,1,0:T(8,128)S(1)} fusion(f32[8,4,128,256,1,1]{3,2,1,0,5,4:T(8,128)} %bitcast.120, pred[2,8,8,4]{2,1,3,0:T(8,128)(4,1)S(1)} %broadcast_compare_fusion, pred[2,8]{1,0:T(4,128)(4,1)S(1)} %iota_compare_fusion), kind=kOutput, calls=%fused_computation.24 | convolution fusion | flops 402654208 | bytes 8389136 | tf_op jit(solution)/shard_map/phqgk,gkbr->phqbr/dot_general | solution.py:95
  194.2 0.4 fusion.64
  194.6 0.6 copy.31
  195.3 0.6 copy-done.7
  195.8 1.3 copy-done.3
  197.2 8.2 %fusion.34 = f32[2,512,256]{1,2,0:T(8,128)} fusion(f32[2,512,1024]{2,1,0:T(8,128)S(1)} %copy-done.3, f32[2,1024,256]{2,1,0:T(8,128)S(1)} %copy-done.7, f32[2,1024,256]{2,1,0:T(8,128)S(1)} %bitcast.127), kind=kOutput, calls=%fused_computation.30 | convolution fusion | flops 3221749760 | bytes 9437184 | tf_op jit(solution)/shard_map/fab,fbr->far/dot_general | solution.py:30
  205.4 49.8 %all-reduce.7.cloned.1.call-done = f32[2,512,256]{1,2,0:T(8,128)} async-done(((f32[2,512,256]{1,2,0:T(8,128)}), f32[2,512,256]{1,2,0:T(8,128)}) %all-reduce.7.cloned.1.call-update) | async-done | bytes 1048592 | tf_op jit(solution)/shard_map/psum | solution.py:22
  255.2 7.5 convolution_bitcast_fusion.4
  262.8 0.1 constant_dynamic-slice_fusion
  262.8 1.9 copy.33
  264.8 1.9 copy.34
  266.7 61.2 %all-reduce.9.cloned.1.call-done = f32[2,1024,256]{1,2,0:T(8,128)} async-done(((f32[2,1024,256]{1,2,0:T(8,128)}), f32[2,1024,256]{1,2,0:T(8,128)}) %all-reduce.9.cloned.1.call-update) | async-done | bytes 2097168 | tf_op jit(solution)/shard_map/psum | solution.py:26
  328.0 2.1 sub.14
  330.0 0.5 copy.59
  330.5 2.0 copy.35
  332.5 3.2 convolution_bitcast_fusion.2
  335.7 0.8 copy.36
  336.6 0.9 copy-done.6
  337.5 0.3 bitcast_add_fusion
  337.8 26.2 %convolution_bitcast_fusion.1 = f32[1280,256]{0,1:T(8,128)} fusion(f32[2560,256]{1,0:T(8,128)S(1)} %bitcast_add_fusion, f32[1280,2560]{1,0:T(8,128)} %param.28), kind=kOutput, calls=%fused_computation.22 | convolution fusion | flops 10066329600 | bytes 17039360 | tf_op jit(solution)/shard_map/dot_general | solution.py:118
  364.1 56.1 %all-reduce.11.cloned.1.call-done = f32[1280,256]{0,1:T(8,128)} async-done(((f32[1280,256]{0,1:T(8,128)}), f32[1280,256]{0,1:T(8,128)}) %all-reduce.11.cloned.1.call-update) | async-done | bytes 1310736 | tf_op jit(solution)/shard_map/psum | solution.py:22
  420.2 15.6 %convolution_bitcast_fusion = f32[2560,256]{0,1:T(8,128)} fusion(f32[1280,256]{0,1:T(8,128)} %all-reduce.11.cloned.1.call-done, f32[2560,1280]{1,0:T(8,128)} %param.29), kind=kOutput, calls=%fused_computation.14 | convolution fusion | flops 10066329600 | bytes 17039360 | tf_op jit(solution)/shard_map/dot_general | solution.py:126
  435.9 69.2 %all-reduce.13.cloned.1.call-done = f32[2560,256]{0,1:T(8,128)} async-done(((f32[2560,256]{0,1:T(8,128)}), f32[2560,256]{0,1:T(8,128)}) %all-reduce.13.cloned.1.call-update) | async-done | bytes 2621456 | tf_op jit(solution)/shard_map/psum | solution.py:26
  505.0 3.2 copy.37
  508.3 4.5 fusion.14
  512.8 0.6 copy.39
  513.4 8.0 %convolution_bitcast_fusion.5 = f32[2,512,256]{1,2,0:T(8,128)} fusion(f32[2,1024,256]{2,1,0:T(8,128)S(1)} %bitcast.123, f32[2,512,1024]{2,1,0:T(8,128)S(1)} %copy-done.2), kind=kOutput, calls=%fused_computation.31 | convolution fusion | flops 3221225472 | bytes 7340032 | tf_op jit(solution)/shard_map/fab,fbr->far/dot_general | solution.py:30
  521.5 0.3 all-reduce.17.cloned.1.call-start
  521.8 51.4 %all-reduce.15.cloned.1.call-done = f32[2,512,256]{1,2,0:T(8,128)} async-done(((f32[2,512,256]{1,2,0:T(8,128)}), f32[2,512,256]{1,2,0:T(8,128)}) %all-reduce.15.cloned.1.call-update) | async-done | bytes 1048592 | tf_op jit(solution)/shard_map/psum | solution.py:22
  573.2 7.5 convolution_bitcast_fusion.3
  580.7 0.6 dynamic_slice.20
  581.4 0.6 iota_compare_fusion.1
  582.1 63.8 %all-reduce.17.cloned.1.call-done = f32[2,1024,256]{1,2,0:T(8,128)} async-done(((f32[2,1024,256]{1,2,0:T(8,128)}), f32[2,1024,256]{1,2,0:T(8,128)}) %all-reduce.17.cloned.1.call-update) | async-done | bytes 2097168 | tf_op jit(solution)/shard_map/psum | solution.py:26
  645.9 2.9 copy.40
  648.8 3.0 copy.41
  651.8 1.9 fusion.37
  653.7 0.1 copy.43
  653.8 8.4 %fusion.23 = f32[2048,256]{0,1:T(8,128)} fusion(f32[512,256]{1,0:T(8,128)S(1)} %bitcast.128, f32[1,2048,512]{2,1,0:T(8,128)S(1)} %copy-done.4), kind=kOutput, calls=%fused_computation.20 | convolution fusion | flops 3221225472 | bytes 6815744 | tf_op jit(solution)/shard_map/dot_general | solution.py:12
  662.2 0.3 reduce-scatter.11.cloned.1.call-start
  662.5 34.6 %reduce-scatter.9.cloned.1.call-done = f32[512,256]{0,1:T(8,128)} async-done(((f32[2048,256]{0,1:T(8,128)}), f32[512,256]{0,1:T(8,128)}) %reduce-scatter.9.cloned.1.call-update) | async-done | bytes 524304 | tf_op jit(solution)/shard_map/reduce_scatter | solution.py:11
  697.1 7.4 fusion.26
  704.5 35.3 %reduce-scatter.11.cloned.1.call-done = f32[512,256]{0,1:T(8,128)} async-done(((f32[2048,256]{0,1:T(8,128)}), f32[512,256]{0,1:T(8,128)}) %reduce-scatter.11.cloned.1.call-update) | async-done | bytes 524304 | tf_op jit(solution)/shard_map/reduce_scatter | solution.py:11
  739.9 1.1 multiply_bitcast_fusion
  740.9 1.0 copy.44
  (65 shorter events, 1.4 us)
Async XLA Ops:
  7.2 146.5 %copy-start = (s32[8,16]{1,0:T(8,128)S(1)}, s32[8,16]{1,0:T(8,128)}, u32[]{:S(2)}) copy-start(s32[8,16]{1,0:T(8,128)} %param.32) | copy-start | bytes 1540
  7.2 50.6 %reduce-scatter.5.cloned.1.call-start = ((), (), s32[]{:S(2)}) async-start(), calls=%async_computation.4 | async-start | bytes 2621440 | tf_op jit(solution)/shard_map/reduce_scatter | solution.py:11
  19.7 134.1 %copy-start.10 = (s32[8]{0:T(128)S(1)}, s32[8]{0:T(128)}, u32[]{:S(2)}) copy-start(s32[8]{0:T(128)} %param.30) | copy-start | bytes 100
  19.7 80.7 %reduce-scatter.7.cloned.1.call-start = ((), (), s32[]{:S(2)}) async-start(), calls=%async_computation.5 | async-start | bytes 2621440 | tf_op jit(solution)/shard_map/reduce_scatter | solution.py:11
  65.1 190.1 %all-reduce.7.cloned.1.call-start = ((), (), s32[]{:S(2)}) async-start(), calls=%async_computation.6 | async-start | bytes 2097152 | tf_op jit(solution)/shard_map/psum | solution.py:22
  100.5 75.7 %copy-start.1 = (f32[512,256]{0,1:T(8,128)S(1)}, f32[512,256]{0,1:T(8,128)}, u32[]{:S(2)}) copy-start(f32[512,256]{0,1:T(8,128)} %reduce-scatter.7.cloned.1.call-done) | copy-start | bytes 1572868
  101.6 10.5 %collective-permute-start = (f32[1,512,256]{1,2,0:T(8,128)S(1)}, f32[1,512,256]{1,2,0:T(8,128)S(1)}, u32[]{:S(2)}, u32[]{:S(2)}) collective-permute-start(f32[1,512,256]{1,2,0:T(8,128)S(1)} %negate_bitcast_fusion), channel_id=1, source_target_pairs={{0,4},{4,8},{8,12},{12,16},{16,20},{20,24},{24,28},{28,0},{1,5},{5... | collective-permute-start | bytes 1572872 | tf_op jit(solution)/shard_map/ppermute | solution.py:88
  112.1 10.4 %collective-permute-start.1 = (f32[1,512,256]{1,2,0:T(8,128)S(1)}, f32[1,512,256]{1,2,0:T(8,128)S(1)}, u32[]{:S(2)}, u32[]{:S(2)}) collective-permute-start(f32[1,512,256]{1,2,0:T(8,128)S(1)} %collective-permute-done), channel_id=1, source_target_pairs={{0,4},{4,8},{8,12},{12,16},{16,20},{20,24},{24,28},{28,0},{1,5},{5... | collective-permute-start | bytes 1572872 | tf_op jit(solution)/shard_map/ppermute | solution.py:88
  122.5 10.4 %collective-permute-start.2 = (f32[1,512,256]{1,2,0:T(8,128)S(1)}, f32[1,512,256]{1,2,0:T(8,128)S(1)}, u32[]{:S(2)}, u32[]{:S(2)}) collective-permute-start(f32[1,512,256]{1,2,0:T(8,128)S(1)} %collective-permute-done.1), channel_id=1, source_target_pairs={{0,4},{4,8},{8,12},{12,16},{16,20},{20,24},{24,28},{28,0},{1,5},{5... | collective-permute-start | bytes 1572872 | tf_op jit(solution)/shard_map/ppermute | solution.py:88
  132.9 10.4 %collective-permute-start.3 = (f32[1,512,256]{1,2,0:T(8,128)S(1)}, f32[1,512,256]{1,2,0:T(8,128)S(1)}, u32[]{:S(2)}, u32[]{:S(2)}) collective-permute-start(f32[1,512,256]{1,2,0:T(8,128)S(1)} %collective-permute-done.2), channel_id=1, source_target_pairs={{0,4},{4,8},{8,12},{12,16},{16,20},{20,24},{24,28},{28,0},{1,5},{5... | collective-permute-start | bytes 1572872 | tf_op jit(solution)/shard_map/ppermute | solution.py:88
  143.3 10.4 %collective-permute-start.4 = (f32[1,512,256]{1,2,0:T(8,128)S(1)}, f32[1,512,256]{1,2,0:T(8,128)S(1)}, u32[]{:S(2)}, u32[]{:S(2)}) collective-permute-start(f32[1,512,256]{1,2,0:T(8,128)S(1)} %collective-permute-done.3), channel_id=1, source_target_pairs={{0,4},{4,8},{8,12},{12,16},{16,20},{20,24},{24,28},{28,0},{1,5},{5... | collective-permute-start | bytes 1572872 | tf_op jit(solution)/shard_map/ppermute | solution.py:88
  153.7 10.5 %collective-permute-start.5 = (f32[1,512,256]{1,2,0:T(8,128)S(1)}, f32[1,512,256]{1,2,0:T(8,128)}, u32[]{:S(2)}, u32[]{:S(2)}) collective-permute-start(f32[1,512,256]{1,2,0:T(8,128)S(1)} %collective-permute-done.4), channel_id=1, source_target_pairs={{0,4},{4,8},{8,12},{12,16},{16,20},{20,24},{24,28},{28,0},{1,5},{5... | collective-permute-start | bytes 1572872 | tf_op jit(solution)/shard_map/ppermute | solution.py:88
  164.2 10.6 %collective-permute-start.6 = (f32[1,512,256]{1,2,0:T(8,128)}, f32[1,512,256]{1,2,0:T(8,128)S(1)}, u32[]{:S(2)}, u32[]{:S(2)}) collective-permute-start(f32[1,512,256]{1,2,0:T(8,128)} %collective-permute-done.5), channel_id=1, source_target_pairs={{0,4},{4,8},{8,12},{12,16},{16,20},{20,24},{24,28},{28,0},{1,5},{5... | collective-permute-start | bytes 1572872 | tf_op jit(solution)/shard_map/ppermute | solution.py:88
  194.2 1.6 copy-start.7
  194.6 2.5 copy-start.3
  205.4 57.4 %copy-start.9 = (s32[2,32]{1,0:T(2,128)S(1)}, s32[2,32]{1,0:T(2,128)}, u32[]{:S(2)}) copy-start(s32[2,32]{1,0:T(2,128)} %param.33) | copy-start | bytes 772
  205.4 122.6 %all-reduce.9.cloned.1.call-start = ((), (), s32[]{:S(2)}) async-start(), calls=%async_computation.7 | async-start | bytes 4194304 | tf_op jit(solution)/shard_map/psum | solution.py:26
  262.7 157.5 %all-reduce.11.cloned.1.call-start = ((), (), s32[]{:S(2)}) async-start(), calls=%async_computation.8 | async-start | bytes 2621440 | tf_op jit(solution)/shard_map/psum | solution.py:22
  335.7 1.7 copy-start.6
  364.0 141.0 %all-reduce.13.cloned.1.call-start = ((), (), s32[]{:S(2)}) async-start(), calls=%async_computation.9 | async-start | bytes 5242880 | tf_op jit(solution)/shard_map/psum | solution.py:26
  435.8 137.4 %all-reduce.15.cloned.1.call-start = ((), (), s32[]{:S(2)}) async-start(), calls=%async_computation.10 | async-start | bytes 2097152 | tf_op jit(solution)/shard_map/psum | solution.py:22
  508.3 5.2 copy-start.2
  513.4 59.8 %copy-start.5 = (f32[2,512,256]{1,2,0:T(8,128)S(1)}, f32[2,512,256]{1,2,0:T(8,128)}, u32[]{:S(2)}) copy-start(f32[2,512,256]{1,2,0:T(8,128)} %all-reduce.7.cloned.1.call-done) | copy-start | bytes 3145732
  521.5 124.4 %all-reduce.17.cloned.1.call-start = ((), (), s32[]{:S(2)}) async-start(), calls=%async_computation.11 | async-start | bytes 4194304 | tf_op jit(solution)/shard_map/psum | solution.py:26
  580.7 116.5 %reduce-scatter.9.cloned.1.call-start = ((), (), s32[]{:S(2)}) async-start(), calls=%async_computation.12 | async-start | bytes 2621440 | tf_op jit(solution)/shard_map/reduce_scatter | solution.py:11
  648.8 5.0 copy-start.4
  653.8 43.3 %copy-start.8 = (f32[512,256]{0,1:T(8,128)S(1)}, f32[512,256]{0,1:T(8,128)}, u32[]{:S(2)}) copy-start(f32[512,256]{0,1:T(8,128)} %reduce-scatter.5.cloned.1.call-done) | copy-start | bytes 1572868
  662.2 77.7 %reduce-scatter.11.cloned.1.call-start = ((), (), s32[]{:S(2)}) async-start(), calls=%async_computation.13 | async-start | bytes 2621440 | tf_op jit(solution)/shard_map/reduce_scatter | solution.py:11
Sparse Core Ops, SparseCore 0:
  19.8 37.9 reduce-scatter.4
  65.2 35.1 reduce-scatter.6
  205.5 49.6 all-reduce.6
  262.8 65.0 all-reduce.8
  364.2 55.9 all-reduce.10
  436.0 69.0 all-reduce.12
  521.6 51.5 all-reduce.14
  580.8 65.0 all-reduce.16
  662.3 34.7 reduce-scatter.8
  704.6 35.1 reduce-scatter.10
